TPU v7x, 128 devices: a whole 4x4x4 slice. The times are simulated.
128 devices in a mesh: row: 16 (over x, y_hi, core), col: 8 (over z, y_lo).
Axes of the slice: x: 4, y: 4 (y_hi: 2, y_lo: 2; y = y_hi * 2 + y_lo), z: 4, core: 2. Of those that a mesh axis runs over, the one named last changes fastest.
Arguments:
- left_pairs: float32 [20480, 1536], P('row', 'col'), may hold values from -6 to 6
- right_pairs: float32 [1536, 20480], P('row', 'col'), may hold values from -0.15625 to 0.15625
- pair_weight: float32 [1536], P('row'), may hold values from 0.3 to 3
- screen: float32 [20480], replicated, may hold values from 6 to 12
- panel_index: int32 [2], replicated, may hold values from 0 to 79, as said below
Outputs:
- dielectric: float32 [20480, 20480], P('row', 'col')
Inputs may be any that keep to these rules, and one draw needn't show every extreme that they name: `panel_index`: two different block indices; one of them, at either section, is the last block 79, the other lies in 0 to 78.
All inputs are finite; a program needn't handle non-finite values.
Results may differ from a plain program's by a relative error of at most 0.0001.
Values sent between devices are 32-bit elements; how exact they have to be, the bound alone decides.
A program may use at most 128 MiB of HBM per device.

v0:
```python
import jax
import jax.numpy as jnp
from jax import lax
from jax.experimental import pallas as pl
from jax.experimental.pallas import tpu as pltpu
from jax.sharding import PartitionSpec as P

PANEL = 256
SECTIONS = 2
NS_STEPS = 3

COUPLING = 0.08

SCHEDULE = (
    "p", "wy", "ly", "w0", "l0", "p", "p", "p", "wy", "ly",
    "w0", "l0", "p", "w0", "l0", "w1", "l1", "p", "w1", "l1",
    "p", "p", "p", "w0", "p", "w0", "w1", "l1", "p", "t",
    "chain", "w1", "w1", "t", "chain",
)

MESH = pl.DeviceIdType.MESH
F32 = jnp.float32
BF = jnp.bfloat16


def remote(src, dst, send_sem, recv_sem, target):
    return pltpu.make_async_remote_copy(
        src_ref=src,
        dst_ref=dst,
        send_sem=send_sem,
        recv_sem=recv_sem,
        device_id=target,
        device_id_type=MESH,
    )


class Ring:
    def __init__(self, ref, me, ahead, behind, send_sems, recv_sems, base):
        self.ref, self.me = ref, me
        self.ahead, self.behind = ahead, behind
        self.send_sems, self.recv_sems, self.base = send_sems, recv_sems, base
        self.sent = []

    def pos(self, step):
        return lax.rem(self.me + 4 + step, 4)

    def send(self, src, pos, half, key, target):
        copy = remote(
            src,
            self.ref(pos, half),
            self.send_sems.at[self.base + key],
            self.recv_sems.at[self.base + key],
            target,
        )
        copy.start()
        self.sent.append(copy)

    def arrived(self, pos, half, key):
        ref = self.ref(pos, half)
        remote(
            ref,
            ref,
            self.send_sems.at[self.base + key],
            self.recv_sems.at[self.base + key],
            self.ahead,
        ).wait_recv()

    def start(self, half_at, source=None):
        source = source or (lambda half: self.ref(self.me, half))
        first, second = (0, 1) if half_at == 0 else (1, 0)
        self.send(source(first), self.me, first, first, self.ahead)
        self.send(source(second), self.me, second, 2 + second, self.behind)

    def forward(self):
        self.arrived(self.pos(-1), 0, 0)
        self.send(self.ref(self.pos(-1), 0), self.pos(-1), 0, 4, self.ahead)
        self.arrived(self.pos(1), 1, 3)
        self.send(self.ref(self.pos(1), 1), self.pos(1), 1, 5, self.behind)

    def finish_near(self):
        self.arrived(self.pos(-1), 1, 1)
        self.arrived(self.pos(1), 0, 2)

    def finish_far(self):
        self.arrived(self.pos(2), 0, 4)
        self.arrived(self.pos(2), 1, 5)

    def drain(self):
        for copy in self.sent:
            copy.wait_send()


def split(a):
    hi = a.astype(BF)
    return hi, (a - hi.astype(F32)).astype(BF)


def dot3(a, b, dims=((1,), (0,))):
    def one(p, q):
        return lax.dot_general(p, q, (dims, ((), ())), preferred_element_type=F32)

    return one(a[0], b[0]) + one(a[0], b[1]) + one(a[1], b[0])


def unit():
    rows = lax.broadcasted_iota(jnp.int32, (PANEL, PANEL), 0)
    cols = lax.broadcasted_iota(jnp.int32, (PANEL, PANEL), 1)
    return (rows == cols).astype(F32)


def newton_inverse(matrix_in):
    eye = unit()
    approx = eye / jnp.sum(matrix_in * eye, axis=0, keepdims=True)
    whole = split(matrix_in)
    for _ in range(NS_STEPS):
        now = split(approx)
        product = dot3(whole, now)
        approx = dot3(now, split(2.0 * eye - product))
    return approx


def gather_kernel(
    left_ref,
    right_ref,
    index_ref,
    screen_ref,
    w_ref,
    high_ref,
    low_ref,
    lower_ref,
    lt,
    p_ref,
    lkt,
    wk,
    lh,
    ll,
    cc,
    lower,
    eh,
    el,
    mids,
    lp_ref,
    wp_ref,
    lp_in,
    wp_in,
    piece,
    own_left,
    own_right,
    send_sems,
    recv_sems,
    lps_sems,
    lpr_sems,
    wps_sems,
    wpr_sems,
    local_sems,
    left_sems,
):
    r = lax.axis_index("row")
    c = lax.axis_index("col")
    core = lax.rem(r, 2)
    yh = lax.rem(r // 2, 2)
    x = r // 4
    yl = lax.rem(c, 2)
    z = c // 2
    y = yh * 2 + yl

    def at(x=x, y=y, z=z, core=core):
        return {"row": (x * 2 + y // 2) * 2 + core, "col": z * 2 + lax.rem(y, 2)}

    x_up, x_down = at(x=lax.rem(x + 1, 4)), at(x=lax.rem(x + 3, 4))
    z_up, z_down = at(z=lax.rem(z + 1, 4)), at(z=lax.rem(z + 3, 4))
    far = at(y=lax.rem(y + 2, 4))
    near = at(y=yh * 2 + 1 - yl)
    other = at(core=1 - core)

    def l_slot(slot, half):
        return lt.at[pl.ds(pl.multiple_of(slot * 192 + half * 96, 96), 96), :]

    own_l = pltpu.make_async_copy(left_ref, own_left, local_sems.at[0])
    own_w = pltpu.make_async_copy(right_ref, own_right, local_sems.at[1])
    own_l.start()
    own_w.start()
    put_w = pltpu.make_async_copy(own_right, w_ref.at[r], local_sems.at[3])
    put_l = pltpu.make_async_copy(
        own_left, lt.at[pl.ds(pl.multiple_of(c * 192, 192), 192), :], local_sems.at[5]
    )

    barrier = pltpu.get_barrier_semaphore()

    def greet_row(k, carry):
        pl.semaphore_signal(
            barrier, 1, device_id={"row": lax.rem(r + k, 16), "col": c}, device_id_type=MESH
        )
        return carry

    def greet_col(k, carry):
        pl.semaphore_signal(
            barrier, 1, device_id={"row": r, "col": lax.rem(c + k, 8)}, device_id_type=MESH
        )
        return carry

    lax.fori_loop(1, 16, greet_row, 0)
    lax.fori_loop(1, 8, greet_col, 0)
    across = at(y=lax.rem(y + 3 + 2 * yl, 4))
    pl.semaphore_signal(barrier, 1, device_id=across, device_id_type=MESH)

    def hit(s, block):
        return jnp.where(index_ref[s : s + 1, :] == block, 1.0, 0.0)

    own_l.wait()
    own_w.wait()
    put_l.start()
    put_w.start()
    for s in range(SECTIONS):
        part = jnp.zeros((192, PANEL), F32)
        for b in range(5):
            part = part + own_left[:, b * PANEL : (b + 1) * PANEL] * hit(s, r * 5 + b)
        for g in range(8):
            lp_ref[g * 2 + s] = part[g * 24 : g * 24 + 24]
        part = jnp.zeros((96, PANEL), F32)
        for b in range(10):
            part = part + own_right[:, b * PANEL : (b + 1) * PANEL] * hit(s, c * 10 + b)
        for g in range(4):
            wp_ref[g * 2 + s] = part[g * 24 : g * 24 + 24]
    pl.semaphore_wait(barrier, 23)

    def lp_copy(k):
        to = lax.rem(r + k, 16)
        return remote(
            lp_ref.at[to], lp_in.at[r], lps_sems.at[k], lpr_sems.at[k], {"row": to, "col": c}
        )

    def wp_copy(k):
        to = lax.rem(c + k, 8)
        return remote(
            wp_ref.at[to], wp_in.at[c], wps_sems.at[k], wpr_sems.at[k], {"row": r, "col": to}
        )

    def w_place(yh_of):
        return lambda pos, half: w_ref.at[(pos * 2 + yh_of) * 2 + core, pl.ds(half * 48, 48), :]

    def l_place(yl_of):
        return lambda pos, half: l_slot(pos * 2 + yl_of, half)

    w_rings = [
        Ring(w_place(yh), x, x_up, x_down, send_sems, recv_sems, 0),
        Ring(w_place(1 - yh), x, x_up, x_down, send_sems, recv_sems, 6),
    ]
    l_rings = [
        Ring(l_place(yl), z, z_up, z_down, send_sems, recv_sems, 12),
        Ring(l_place(1 - yl), z, z_up, z_down, send_sems, recv_sems, 18),
    ]
    pz = Ring(
        lambda pos, half: p_ref.at[core, y, x, pos, pl.ds(half * 24, 24), :],
        z, z_up, z_down, send_sems, recv_sems, 36,
    )
    px = Ring(
        lambda pos, half: p_ref.at[core, y, pos, pl.ds(half * 2, 2)],
        x, x_up, x_down, send_sems, recv_sems, 42,
    )
    spots = [x, px.pos(-1), px.pos(1), px.pos(2)]

    def w_own(half):
        return right_ref.at[pl.ds(half * 48, 48), :]

    def l_own(half):
        return left_ref.at[pl.ds(half * 96, 96), :]

    swaps = []

    def swap(src, dst, key, target):
        copy = remote(src, dst, send_sems.at[key], recv_sems.at[key], target)
        copy.start()
        swaps.append(copy)

    def to_other(pos, yh_of, key):
        slot = w_ref.at[(pos * 2 + yh_of) * 2 + core]
        swap(slot, slot, key, other)

    def arrived(ref, key):
        remote(ref, ref, send_sems.at[key], recv_sems.at[key], other).wait_recv()

    def from_other(pos, yh_of, key):
        arrived(w_ref.at[(pos * 2 + yh_of) * 2 + 1 - core], key)

    def flow_w0():
        ring = w_rings[0]
        ring.start(0, w_own)
        yield
        ring.start(1, w_own)
        yield
        swap(own_right, w_ref.at[r], 28, other)
        ring.forward()
        yield
        ring.finish_near()
        to_other(ring.pos(-1), yh, 30)
        to_other(ring.pos(1), yh, 31)
        yield
        ring.finish_far()
        to_other(ring.pos(2), yh, 32)
        yield

    def flow_wy():
        for half in range(2):
            swap(w_own(half), w_place(yh)(x, half), 24 + half, far)
            yield

    def follow(ring, place, me, key):
        for half in range(2):
            ref = place(me, half)
            arrived(ref, key + half)
            ring.send(ref, me, half, half, ring.ahead)
            ring.send(ref, me, half, 2 + half, ring.behind)
            yield

    def flow_w1():
        ring = w_rings[1]
        yield from follow(ring, w_place(1 - yh), x, 24)
        to_other(x, 1 - yh, 29)
        ring.forward()
        yield
        ring.finish_near()
        to_other(ring.pos(-1), 1 - yh, 33)
        to_other(ring.pos(1), 1 - yh, 34)
        yield
        ring.finish_far()
        to_other(ring.pos(2), 1 - yh, 35)
        yield

    def flow_l0():
        ring = l_rings[0]
        ring.start(0, l_own)
        yield
        ring.start(1, l_own)
        yield
        ring.forward()
        yield

    def flow_ly():
        for half in range(2):
            swap(l_own(half), l_place(yl)(z, half), 26 + half, near)
            yield

    def flow_l1():
        ring = l_rings[1]
        yield from follow(ring, l_place(1 - yl), z, 26)
        ring.forward()
        yield

    def turn(pos):
        at_k = pl.ds(pl.multiple_of(pos * 384, 384), 384)

        @pl.loop(0, 5)
        def _(m):
            at_m = pl.ds(pl.multiple_of(m * PANEL, PANEL), PANEL)
            hi, lo = split(lt[at_k, at_m].T)
            lh[at_m, at_k] = hi
            ll[at_m, at_k] = lo

    def flow_t():
        put_l.wait()
        for ring in l_rings:
            ring.finish_near()
        for step in (0, -1, 1):
            turn(l_rings[0].pos(step))
        yield
        for ring in l_rings:
            ring.finish_far()
        turn(l_rings[0].pos(2))
        yield

    def flow_p():
        for k in range(1, 16):
            lp_copy(k).start()
        for k in range(1, 8):
            wp_copy(k).start()
        yield
        total_l = lp_ref[r]
        for k in range(1, 16):
            lp_copy(k).wait_recv()
        for k in range(1, 16):
            total_l = total_l + lp_in[lax.rem(r + 16 - k, 16)]
        total_w = wp_ref[c]
        for k in range(1, 8):
            wp_copy(k).wait_recv()
        for k in range(1, 8):
            total_w = total_w + wp_in[lax.rem(c + 8 - k, 8)]
        piece[pl.ds(0, 24), :] = total_l
        piece[pl.ds(24, 24), :] = total_w
        own_p = pltpu.make_async_copy(piece, p_ref.at[core, y, x, z], local_sems.at[2])
        own_p.start()
        for half in range(2):
            pz.start(half, lambda h: piece.at[pl.ds(h * 24, 24), :])
        yield
        pz.forward()
        yield
        def slot(y_of, i):
            return p_ref.at[core, y_of, spots[i]]

        def go(i):
            swap(slot(y, i), slot(y, i), 55 + 3 * i, near)
            swap(slot(y, i), slot(y, i), 56 + 3 * i, across)

        def onward(i):
            ref = slot(yh * 2 + 1 - yl, i)
            arrived(ref, 55 + 3 * i)
            swap(ref, ref, 57 + 3 * i, across)

        def share(i):
            arrived(slot(lax.rem(y + 3 + 2 * yl, 4), i), 56 + 3 * i)
            arrived(slot(lax.rem(y + 2, 4), i), 57 + 3 * i)
            whole = p_ref.at[core, pl.ds(0, 4), spots[i]]
            swap(whole, whole, 67 + i, other)

        own_p.wait()
        pz.finish_near()
        pz.finish_far()
        for half in range(2):
            px.start(half)
        go(0)
        yield
        px.forward()
        yield
        px.finish_near()
        go(1)
        go(2)
        onward(0)
        yield
        px.finish_far()
        go(3)
        onward(1)
        onward(2)
        yield
        share(0)
        onward(3)
        yield
        share(1)
        share(2)
        yield
        share(3)
        yield
        for i in range(4):
            arrived(p_ref.at[1 - core, pl.ds(0, 4), spots[i]], 67 + i)
        place_panels()
        yield

    def place_panels():
        @pl.loop(0, 32)
        def _(i):
            x_of, yh_of, z_of = i // 8, lax.rem(i // 4, 2), lax.rem(i, 4)
            for core_of in range(2):
                for yl_of in range(2):
                    block = p_ref[core_of, yh_of * 2 + yl_of, x_of, z_of]
                    at_l = pl.multiple_of((z_of * 2 + yl_of) * 192 + (x_of * 2 + yh_of) * 24, 24)
                    at_w = pl.multiple_of(
                        ((x_of * 2 + yh_of) * 2 + core_of) * 96 + z_of * 24, 24
                    )
                    lkt[pl.ds(at_l, 24), pl.ds(core_of * PANEL, PANEL)] = block[:24]
                    wk[pl.ds(at_w, 24), pl.ds(yl_of * PANEL, PANEL)] = block[24:]

    first, second = pl.ds(0, PANEL), pl.ds(PANEL, PANEL)

    def flow_chain():
        mids[...] = jnp.zeros_like(mids)

        @pl.loop(0, 6)
        def _(k):
            at_k = pl.ds(pl.multiple_of(k * PANEL, PANEL), PANEL)
            mids[...] += COUPLING * dot3(split(lkt[at_k, :].T), split(wk[at_k, :]))

        def screened(block, s):
            places = lax.broadcasted_iota(jnp.int32, (80, PANEL), 0)
            chosen = jnp.where(places == index_ref[s : s + 1, :], screen_ref[...], 0.0)
            return block + unit() * jnp.sum(chosen, axis=0, keepdims=True)

        inv1 = split(newton_inverse(screened(mids[first, first], 0)))
        x12 = split(mids[first, second])
        b1 = split(dot3(split(mids[second, first]), inv1))
        inv2 = split(newton_inverse(screened(mids[second, second] - dot3(b1, x12), 1)))
        yield
        for half in (first, second):
            cc[:, half] = COUPLING * dot3((lh[...], ll[...]), split(wk[:, half]))

        @pl.loop(0, 5)
        def _(m):
            at_m = pl.ds(pl.multiple_of(m * PANEL, PANEL), PANEL)
            mask1 = 1.0 - hit(0, r * 5 + m)
            mask2 = mask1 * (1.0 - hit(1, r * 5 + m))
            low1 = dot3(split(cc[at_m, first]), inv1) * mask1
            low2 = cc[at_m, second] - dot3(split(low1), x12)
            low2 = dot3(split(low2), inv2) * mask2
            lower[at_m, first] = low1
            lower[at_m, second] = low2
            pair = split(low2)
            eh[at_m, second], el[at_m, second] = pair
            eh[at_m, first], el[at_m, first] = split(low1 - dot3(pair, b1))

        put_lower.start()

        @pl.loop(0, 6)
        def _(k):
            at_k = pl.ds(pl.multiple_of(k * PANEL, PANEL), PANEL)
            panel = split(lkt[at_k, :])
            now = lh[:, at_k].astype(F32) + ll[:, at_k].astype(F32)
            now = now - dot3((eh[...], el[...]), panel, ((1,), (1,)))
            lh[:, at_k], ll[:, at_k] = split(now)
            for put in put_left(k):
                put.start()

        yield

    def put_left(k):
        at_k = pl.ds(pl.multiple_of(k * PANEL, PANEL), PANEL)
        return (
            pltpu.make_async_copy(lh.at[:, at_k], high_ref.at[:, at_k], left_sems.at[0, k]),
            pltpu.make_async_copy(ll.at[:, at_k], low_ref.at[:, at_k], left_sems.at[1, k]),
        )

    put_lower = pltpu.make_async_copy(lower, lower_ref, local_sems.at[4])

    makers = {
        "w0": flow_w0, "wy": flow_wy, "w1": flow_w1, "l0": flow_l0, "ly": flow_ly,
        "l1": flow_l1, "p": flow_p, "t": flow_t, "chain": flow_chain,
    }
    flows = {}
    for name in SCHEDULE:
        if name not in flows:
            flows[name] = makers[name]()
        next(flows[name])
    for flow in flows.values():
        for _ in flow:
            pass

    ring = w_rings[0]
    from_other(x, yh, 28)
    from_other(x, 1 - yh, 29)
    from_other(ring.pos(-1), yh, 30)
    from_other(ring.pos(1), yh, 31)
    from_other(ring.pos(2), yh, 32)
    from_other(ring.pos(-1), 1 - yh, 33)
    from_other(ring.pos(1), 1 - yh, 34)
    from_other(ring.pos(2), 1 - yh, 35)
    put_w.wait()
    put_lower.wait()
    for k in range(6):
        for put in put_left(k):
            put.wait()
    for k in range(1, 16):
        lp_copy(k).wait_send()
    for k in range(1, 8):
        wp_copy(k).wait_send()
    for ring in w_rings + l_rings + [pz, px]:
        ring.drain()
    for copy in swaps:
        copy.wait_send()


def gather(left_t, right, index, screen):
    any_spec = pl.BlockSpec(memory_space=pl.ANY)
    vmem_spec = pl.BlockSpec(memory_space=pltpu.VMEM)
    dma = pltpu.SemaphoreType.DMA
    return pl.pallas_call(
        gather_kernel,
        out_shape=(
            jax.ShapeDtypeStruct((16, 96, 2560), F32),
            jax.ShapeDtypeStruct((1280, 1536), BF),
            jax.ShapeDtypeStruct((1280, 1536), BF),
            jax.ShapeDtypeStruct((1280, 512), F32),
        ),
        in_specs=[any_spec, any_spec, vmem_spec, vmem_spec],
        out_specs=(any_spec, any_spec, any_spec, any_spec),
        scratch_shapes=[
            pltpu.VMEM((1536, 1280), F32),
            pltpu.VMEM((2, 4, 4, 4, 48, PANEL), F32),
            pltpu.VMEM((1536, 512), F32),
            pltpu.VMEM((1536, 512), F32),
            pltpu.VMEM((1280, 1536), BF),
            pltpu.VMEM((1280, 1536), BF),
            pltpu.VMEM((1280, 512), F32),
            pltpu.VMEM((1280, 512), F32),
            pltpu.VMEM((1280, 512), BF),
            pltpu.VMEM((1280, 512), BF),
            pltpu.VMEM((512, 512), F32),
            pltpu.VMEM((16, 24, PANEL), F32),
            pltpu.VMEM((8, 24, PANEL), F32),
            pltpu.VMEM((16, 24, PANEL), F32),
            pltpu.VMEM((8, 24, PANEL), F32),
            pltpu.VMEM((48, PANEL), F32),
            pltpu.VMEM((192, 1280), F32),
            pltpu.VMEM((96, 2560), F32),
            dma((71,)),
            dma((71,)),
            dma((16,)),
            dma((16,)),
            dma((8,)),
            dma((8,)),
            dma((6,)),
            dma((2, 6)),
        ],
        compiler_params=pltpu.CompilerParams(
            collective_id=0, has_side_effects=True, vmem_limit_bytes=58 << 20
        ),
        name="exchange",
    )(left_t, right, index, screen)


def product_kernel(index_ref, lh_ref, ll_ref, w_ref, lower_ref, screen_ref, o_ref):
    n = pl.program_id(0)
    w = split(w_ref[...])
    o_ref[...] = COUPLING * dot3((lh_ref[...], ll_ref[...]), w)
    row0 = lax.axis_index("row") * 5
    block = lax.axis_index("col") * 10 + n
    rel = block - row0

    @pl.when((rel >= 0) & (rel < 5))
    def _():
        at = pl.ds(pl.multiple_of(rel * PANEL, PANEL), PANEL)
        o_ref[at, :] += unit() * screen_ref[pl.ds(block, 1), :]

    for s in range(2):

        @pl.when(block == index_ref[s])
        def _():
            for m in range(5):
                hit = row0 + m == index_ref[0]
                if s == 1:
                    hit = hit | (row0 + m == index_ref[1])

                @pl.when(jnp.logical_not(hit))
                def _():
                    at = pl.ds(m * PANEL, PANEL)
                    o_ref[at, :] = lower_ref[at, s * PANEL : (s + 1) * PANEL]


def product(index, lh, ll, w, lower, screen):
    once = dict(pipeline_mode=pl.Buffered(1))
    return pl.pallas_call(
        product_kernel,
        out_shape=jax.ShapeDtypeStruct((1280, 2560), F32),
        grid_spec=pltpu.PrefetchScalarGridSpec(
            num_scalar_prefetch=1,
            grid=(10,),
            in_specs=[
                pl.BlockSpec((1280, 1536), lambda n, s: (0, 0), **once),
                pl.BlockSpec((1280, 1536), lambda n, s: (0, 0), **once),
                pl.BlockSpec((1536, PANEL), lambda n, s: (0, n)),
                pl.BlockSpec((1280, 512), lambda n, s: (0, 0), **once),
                pl.BlockSpec((80, PANEL), lambda n, s: (0, 0), **once),
            ],
            out_specs=pl.BlockSpec((1280, PANEL), lambda n, s: (0, n)),
        ),
        compiler_params=pltpu.CompilerParams(vmem_limit_bytes=56 << 20),
        name="product",
    )(index, lh, ll, w, lower, screen)


def shards(left_pairs, right_pairs, pair_weight, screen, panel_index):
    weighted = right_pairs * pair_weight[:, None]
    screen = screen.reshape(80, PANEL)
    index = jnp.broadcast_to(panel_index[:, None], (SECTIONS, PANEL))
    w_all, lh, ll, lower = gather(left_pairs.T, weighted, index, screen)
    return product(panel_index, lh, ll, w_all.reshape(1536, 2560), lower, screen)


def solution(mesh):
    return jax.shard_map(
        shards,
        mesh=mesh,
        in_specs=(P("row", "col"), P("row", "col"), P("row"), P(), P()),
        out_specs=P("row", "col"),
        check_vma=False,
    )
```

profile of v0, /device:TPU:1, one launch (start us, length us, event | category | flops | bytes accessed | tf_op | source)
XLA Modules:
  0.0 165.0 jit_solution(12872105464847925354)
XLA Ops:
  0.0 1.3 broadcast_in_dim.2.index_ref
  1.3 1.5 reshape.8.screen_ref
  2.8 2.3 %broadcast_multiply_fusion.right_ref = f32[96,2560]{1,0:T(8,128)} fusion(f32[96,2560]{1,0:T(8,128)} %param.6, f32[96]{0:T(128)} %param.7), kind=kLoop, calls=%fused_computation | loop fusion | flops 245760 | bytes 1966464 | tf_op jit(solution)/shard_map/mul | solution.py:658
  5.1 120.4 %exchange.1 = (f32[16,96,2560]{2,1,0:T(8,128)}, bf16[1280,1536]{1,0:T(8,128)(2,1)}, bf16[1280,1536]{1,0:T(8,128)(2,1)}, f32[1280,512]{1,0:T(8,128)}) custom-call(f32[192,1280]{1,0:T(8,128)} %bitcast.3, f32[96,2560]{1,0:T(8,128)} %broadcast_multiply_fusion.right_ref, s32[2,256]{1,0:T(2,128)} %broadcast_in_dim.2.index_ref, f32[80,256]{1,0:T(8,128)} %reshape.8.screen_ref), custom_call_target="tpu_custom_call" | custom-call | tf_op jit(solution)/shard_map/exchange/pallas_call | solution.py:562
  125.5 39.5 %product.1 = f32[1280,2560]{1,0:T(8,128)} custom-call(s32[2]{0:T(128)} %index_ref.1, bf16[1280,1536]{1,0:T(8,128)(2,1)} %get-tuple-element.9.lh_ref, bf16[1280,1536]{1,0:T(8,128)(2,1)} %get-tuple-element.10.ll_ref, f32[1536,2560]{1,0:T(8,128)} %bitcast.2, f32[1280,512]{1,0:T(8,128)} %get-tuple-element.12.lower_ref, f32[80,256]{1,0:T(8,128)} %reshape.8.screen_ref), custom_call_target="tpu_custom_call" | custom-call | tf_op jit(solution)/shard_map/product/pallas_call | solution.py:637
where the time goes:
time: 165 us
  Pallas kernels  160 us (97%)
  local copies, waits for them, and re-layouts  2.85 us (2%)
  other arithmetic  2.28 us (1%)
    pallas_call x1, Pallas kernels, gather(): pl.pallas_call(gather_kernel, out_shape=(jax.ShapeDtypeStruct((16, 96, 25...  120 us
    pallas_call x1, Pallas kernels, product(): pl.pallas_call(product_kernel, out_shape=jax.ShapeDtypeStruct((1280, 2560...  39.5 us

commit v1 on v0

--- a/solution.py
+++ b/solution.py
@@ -15,7 +15,8 @@
     "p", "wy", "ly", "w0", "l0", "p", "p", "p", "wy", "ly",
     "w0", "l0", "p", "w0", "l0", "w1", "l1", "p", "w1", "l1",
     "p", "p", "p", "w0", "p", "w0", "w1", "l1", "p", "t",
-    "chain", "w1", "w1", "t", "chain",
+    "c", "c", "p", "c", "p", "chain", "w1", "w1", "t", "c",
+    "chain",
 )
 
 MESH = pl.DeviceIdType.MESH
@@ -394,71 +395,104 @@
         yield
         pz.forward()
         yield
-        def slot(y_of, i):
-            return p_ref.at[core, y_of, spots[i]]
-
-        def go(i):
-            swap(slot(y, i), slot(y, i), 55 + 3 * i, near)
-            swap(slot(y, i), slot(y, i), 56 + 3 * i, across)
-
-        def onward(i):
-            ref = slot(yh * 2 + 1 - yl, i)
-            arrived(ref, 55 + 3 * i)
-            swap(ref, ref, 57 + 3 * i, across)
-
-        def share(i):
-            arrived(slot(lax.rem(y + 3 + 2 * yl, 4), i), 56 + 3 * i)
-            arrived(slot(lax.rem(y + 2, 4), i), 57 + 3 * i)
-            whole = p_ref.at[core, pl.ds(0, 4), spots[i]]
-            swap(whole, whole, 67 + i, other)
+        def slot(part, y_of, i):
+            return p_ref.at[core, y_of, spots[i], :, pl.ds(part * 24, 24), :]
+
+        def go(part, i):
+            ref, key = slot(part, y, i), 48 + 12 * part + 3 * i
+            swap(ref, ref, key, near)
+            swap(ref, ref, key + 1, across)
+
+        def onward(part, i):
+            ref, key = slot(part, yh * 2 + 1 - yl, i), 48 + 12 * part + 3 * i
+            arrived(ref, key)
+            swap(ref, ref, key + 2, across)
+
+        def both(core_of, part, i):
+            return p_ref.at[core_of, pl.ds(0, 4), spots[i], :, pl.ds(part * 24, 24), :]
+
+        def share(part, i):
+            key = 48 + 12 * part + 3 * i
+            arrived(slot(part, lax.rem(y + 3 + 2 * yl, 4), i), key + 1)
+            arrived(slot(part, lax.rem(y + 2, 4), i), key + 2)
+            swap(both(core, part, i), both(core, part, i), 72 + 4 * part + i, other)
 
         own_p.wait()
         pz.finish_near()
         pz.finish_far()
         for half in range(2):
             px.start(half)
-        go(0)
+        go(1, 0)
         yield
         px.forward()
         yield
         px.finish_near()
-        go(1)
-        go(2)
-        onward(0)
+        go(1, 1)
+        go(1, 2)
+        onward(1, 0)
         yield
         px.finish_far()
-        go(3)
-        onward(1)
-        onward(2)
-        yield
-        share(0)
-        onward(3)
-        yield
-        share(1)
-        share(2)
-        yield
-        share(3)
-        yield
+        go(1, 3)
+        onward(1, 1)
+        onward(1, 2)
         for i in range(4):
-            arrived(p_ref.at[1 - core, pl.ds(0, 4), spots[i]], 67 + i)
-        place_panels()
-        yield
-
-    def place_panels():
+            go(0, i)
+        yield
+        share(1, 0)
+        onward(1, 3)
+        onward(0, 0)
+        yield
+        share(1, 1)
+        share(1, 2)
+        onward(0, 1)
+        onward(0, 2)
+        yield
+        share(1, 3)
+        onward(0, 3)
+        share(0, 0)
+        yield
+        for i in range(4):
+            arrived(both(1 - core, 1, i), 76 + i)
+        place(1)
+        yield
+        for i in range(1, 4):
+            share(0, i)
+        yield
+        for i in range(4):
+            arrived(both(1 - core, 0, i), 72 + i)
+        place(0)
+        yield
+
+    def place(part):
         @pl.loop(0, 32)
         def _(i):
             x_of, yh_of, z_of = i // 8, lax.rem(i // 4, 2), lax.rem(i, 4)
             for core_of in range(2):
                 for yl_of in range(2):
-                    block = p_ref[core_of, yh_of * 2 + yl_of, x_of, z_of]
-                    at_l = pl.multiple_of((z_of * 2 + yl_of) * 192 + (x_of * 2 + yh_of) * 24, 24)
-                    at_w = pl.multiple_of(
-                        ((x_of * 2 + yh_of) * 2 + core_of) * 96 + z_of * 24, 24
-                    )
-                    lkt[pl.ds(at_l, 24), pl.ds(core_of * PANEL, PANEL)] = block[:24]
-                    wk[pl.ds(at_w, 24), pl.ds(yl_of * PANEL, PANEL)] = block[24:]
+                    block = p_ref[
+                        core_of, yh_of * 2 + yl_of, x_of, z_of, part * 24 : part * 24 + 24, :
+                    ]
+                    if part == 0:
+                        at_k = (z_of * 2 + yl_of) * 192 + (x_of * 2 + yh_of) * 24
+                        lanes = pl.ds(core_of * PANEL, PANEL)
+                        lkt[pl.ds(pl.multiple_of(at_k, 24), 24), lanes] = block
+                    else:
+                        at_k = ((x_of * 2 + yh_of) * 2 + core_of) * 96 + z_of * 24
+                        lanes = pl.ds(yl_of * PANEL, PANEL)
+                        wk[pl.ds(pl.multiple_of(at_k, 24), 24), lanes] = block
 
     first, second = pl.ds(0, PANEL), pl.ds(PANEL, PANEL)
+
+    def flow_c():
+        for n, step in enumerate((0, -1, 1, 2)):
+            at_k = pl.ds(pl.multiple_of(l_rings[0].pos(step) * 384, 384), 384)
+            for half in (first, second):
+                part = COUPLING * dot3((lh[:, at_k], ll[:, at_k]), split(wk[at_k, half]))
+                if n == 0:
+                    cc[:, half] = part
+                else:
+                    cc[:, half] += part
+            yield
 
     def flow_chain():
         mids[...] = jnp.zeros_like(mids)
@@ -478,8 +512,6 @@
         b1 = split(dot3(split(mids[second, first]), inv1))
         inv2 = split(newton_inverse(screened(mids[second, second] - dot3(b1, x12), 1)))
         yield
-        for half in (first, second):
-            cc[:, half] = COUPLING * dot3((lh[...], ll[...]), split(wk[:, half]))
 
         @pl.loop(0, 5)
         def _(m):
@@ -520,7 +552,7 @@
 
     makers = {
         "w0": flow_w0, "wy": flow_wy, "w1": flow_w1, "l0": flow_l0, "ly": flow_ly,
-        "l1": flow_l1, "p": flow_p, "t": flow_t, "chain": flow_chain,
+        "l1": flow_l1, "p": flow_p, "t": flow_t, "c": flow_c, "chain": flow_chain,
     }
     flows = {}
     for name in SCHEDULE:
@@ -588,8 +620,8 @@
             pltpu.VMEM((48, PANEL), F32),
             pltpu.VMEM((192, 1280), F32),
             pltpu.VMEM((96, 2560), F32),
-            dma((71,)),
-            dma((71,)),
+            dma((80,)),
+            dma((80,)),
             dma((16,)),
             dma((16,)),
             dma((8,)),

time: 165 us -> 167 us (1.012)
  Pallas kernels: 160 us -> 162 us
    pallas_call x1, Pallas kernels: 120 us -> 123 us  [gather(): pl.pallas_call(gather_kernel, out_shape=(jax.ShapeDtypeStruct((16, 96, 25...]
where the time goes in v1:
time: 167 us
  Pallas kernels  162 us (97%)
  local copies, waits for them, and re-layouts  2.85 us (2%)
  other arithmetic  2.28 us (1%)
    pallas_call x1, Pallas kernels, gather(): pl.pallas_call(gather_kernel, out_shape=(jax.ShapeDtypeStruct((16, 96, 25...  123 us
    pallas_call x1, Pallas kernels, product(): pl.pallas_call(product_kernel, out_shape=jax.ShapeDtypeStruct((1280, 2560...  39.2 us

profile of v1, /device:TPU:1, one launch (start us, length us, event | category | flops | bytes accessed | tf_op | source)
XLA Modules:
  0.0 167.1 jit_solution(14394754096233221202)
XLA Ops:
  0.0 1.3 broadcast_in_dim.2.index_ref
  1.3 1.5 reshape.8.screen_ref
  2.8 2.3 %broadcast_multiply_fusion.right_ref = f32[96,2560]{1,0:T(8,128)} fusion(f32[96,2560]{1,0:T(8,128)} %param.6, f32[96]{0:T(128)} %param.7), kind=kLoop, calls=%fused_computation | loop fusion | flops 245760 | bytes 1966464 | tf_op jit(solution)/shard_map/mul | solution.py:690
  5.1 122.8 %exchange.1 = (f32[16,96,2560]{2,1,0:T(8,128)}, bf16[1280,1536]{1,0:T(8,128)(2,1)}, bf16[1280,1536]{1,0:T(8,128)(2,1)}, f32[1280,512]{1,0:T(8,128)}) custom-call(f32[192,1280]{1,0:T(8,128)} %bitcast.3, f32[96,2560]{1,0:T(8,128)} %broadcast_multiply_fusion.right_ref, s32[2,256]{1,0:T(2,128)} %broadcast_in_dim.2.index_ref, f32[80,256]{1,0:T(8,128)} %reshape.8.screen_ref), custom_call_target="tpu_custom_call" | custom-call | tf_op jit(solution)/shard_map/exchange/pallas_call | solution.py:594
  127.9 39.2 %product.1 = f32[1280,2560]{1,0:T(8,128)} custom-call(s32[2]{0:T(128)} %index_ref.1, bf16[1280,1536]{1,0:T(8,128)(2,1)} %get-tuple-element.9.lh_ref, bf16[1280,1536]{1,0:T(8,128)(2,1)} %get-tuple-element.10.ll_ref, f32[1536,2560]{1,0:T(8,128)} %bitcast.2, f32[1280,512]{1,0:T(8,128)} %get-tuple-element.12.lower_ref, f32[80,256]{1,0:T(8,128)} %reshape.8.screen_ref), custom_call_target="tpu_custom_call" | custom-call | tf_op jit(solution)/shard_map/product/pallas_call | solution.py:669

commit v2 on v0

--- a/solution.py
+++ b/solution.py
@@ -122,6 +122,7 @@
 def gather_kernel(
     left_ref,
     right_ref,
+    weight_ref,
     index_ref,
     screen_ref,
     w_ref,
@@ -205,10 +206,15 @@
     pl.semaphore_signal(barrier, 1, device_id=across, device_id_type=MESH)
 
     def hit(s, block):
-        return jnp.where(index_ref[s : s + 1, :] == block, 1.0, 0.0)
+        return jnp.where(index_ref[:, s : s + 1] == block, 1.0, 0.0)
 
     own_l.wait()
     own_w.wait()
+    square = lax.broadcasted_iota(jnp.int32, (96, 96), 0) == lax.broadcasted_iota(
+        jnp.int32, (96, 96), 1
+    )
+    weights = jnp.sum(jnp.where(square, weight_ref[...], 0.0), axis=1, keepdims=True)
+    own_right[...] = own_right[...] * weights
     put_l.start()
     put_w.start()
     for s in range(SECTIONS):
@@ -261,7 +267,7 @@
     spots = [x, px.pos(-1), px.pos(1), px.pos(2)]
 
     def w_own(half):
-        return right_ref.at[pl.ds(half * 48, 48), :]
+        return own_right.at[pl.ds(half * 48, 48), :]
 
     def l_own(half):
         return left_ref.at[pl.ds(half * 96, 96), :]
@@ -470,7 +476,7 @@
 
         def screened(block, s):
             places = lax.broadcasted_iota(jnp.int32, (80, PANEL), 0)
-            chosen = jnp.where(places == index_ref[s : s + 1, :], screen_ref[...], 0.0)
+            chosen = jnp.where(places == index_ref[:, s : s + 1], screen_ref[...], 0.0)
             return block + unit() * jnp.sum(chosen, axis=0, keepdims=True)
 
         inv1 = split(newton_inverse(screened(mids[first, first], 0)))
@@ -555,7 +561,7 @@
         copy.wait_send()
 
 
-def gather(left_t, right, index, screen):
+def gather(left_t, right, weight, index, screen):
     any_spec = pl.BlockSpec(memory_space=pl.ANY)
     vmem_spec = pl.BlockSpec(memory_space=pltpu.VMEM)
     dma = pltpu.SemaphoreType.DMA
@@ -567,7 +573,7 @@
             jax.ShapeDtypeStruct((1280, 1536), BF),
             jax.ShapeDtypeStruct((1280, 512), F32),
         ),
-        in_specs=[any_spec, any_spec, vmem_spec, vmem_spec],
+        in_specs=[any_spec, any_spec, vmem_spec, vmem_spec, vmem_spec],
         out_specs=(any_spec, any_spec, any_spec, any_spec),
         scratch_shapes=[
             pltpu.VMEM((1536, 1280), F32),
@@ -601,7 +607,7 @@
             collective_id=0, has_side_effects=True, vmem_limit_bytes=58 << 20
         ),
         name="exchange",
-    )(left_t, right, index, screen)
+    )(left_t, right, weight, index, screen)
 
 
 def product_kernel(index_ref, lh_ref, ll_ref, w_ref, lower_ref, screen_ref, o_ref):
@@ -655,10 +661,14 @@
 
 
 def shards(left_pairs, right_pairs, pair_weight, screen, panel_index):
-    weighted = right_pairs * pair_weight[:, None]
     screen = screen.reshape(80, PANEL)
-    index = jnp.broadcast_to(panel_index[:, None], (SECTIONS, PANEL))
-    w_all, lh, ll, lower = gather(left_pairs.T, weighted, index, screen)
+    w_all, lh, ll, lower = gather(
+        left_pairs.T,
+        right_pairs,
+        pair_weight.reshape(1, 96),
+        panel_index.reshape(1, SECTIONS),
+        screen,
+    )
     return product(panel_index, lh, ll, w_all.reshape(1536, 2560), lower, screen)
 
 

time: 165 us -> 162 us (0.982)
  other arithmetic: 2.28 us -> 0 us
    mul x1 -> x0, other arithmetic: 2.28 us -> none  [shards(): weighted = right_pairs * pair_weight[:, None]]
where the time goes in v2:
time: 162 us; the launch traced here: 161 us
  Pallas kernels  160 us (99%)
    pallas_call x1, Pallas kernels, gather(): pl.pallas_call(gather_kernel, out_shape=(jax.ShapeDtypeStruct((16, 96, 25...  120 us
    pallas_call x1, Pallas kernels, product(): pl.pallas_call(product_kernel, out_shape=jax.ShapeDtypeStruct((1280, 2560...  39.4 us

profile of v2, /device:TPU:1, one launch (start us, length us, event | category | flops | bytes accessed | tf_op | source)
XLA Modules:
  0.0 161.4 jit_solution(18027474661013632787)
XLA Ops:
  0.0 1.5 reshape.14.screen_ref
  1.5 120.5 %exchange.1 = (f32[16,96,2560]{2,1,0:T(8,128)}, bf16[1280,1536]{1,0:T(8,128)(2,1)}, bf16[1280,1536]{1,0:T(8,128)(2,1)}, f32[1280,512]{1,0:T(8,128)}) custom-call(f32[192,1280]{1,0:T(8,128)} %bitcast.5, f32[96,2560]{1,0:T(8,128)} %right_ref.1, f32[1,96]{1,0:T(1,128)} %bitcast.7, s32[1,2]{1,0:T(1,128)} %bitcast.6, f32[80,256]{1,0:T(8,128)} %reshape.14.screen_ref), custom_call_target="tpu_custom_call" | custom-call | tf_op jit(solution)/shard_map/exchange/pallas_call | solution.py:568
  122.0 39.4 %product.1 = f32[1280,2560]{1,0:T(8,128)} custom-call(s32[2]{0:T(128)} %index_ref.1, bf16[1280,1536]{1,0:T(8,128)(2,1)} %get-tuple-element.9.lh_ref, bf16[1280,1536]{1,0:T(8,128)(2,1)} %get-tuple-element.10.ll_ref, f32[1536,2560]{1,0:T(8,128)} %bitcast.4, f32[1280,512]{1,0:T(8,128)} %get-tuple-element.12.lower_ref, f32[80,256]{1,0:T(8,128)} %reshape.14.screen_ref), custom_call_target="tpu_custom_call" | custom-call | tf_op jit(solution)/shard_map/product/pallas_call | solution.py:643

commit v3 on v2

--- a/solution.py
+++ b/solution.py
@@ -14,7 +14,7 @@
 SCHEDULE = (
     "p", "wy", "ly", "w0", "l0", "p", "p", "p", "wy", "ly",
     "w0", "l0", "p", "w0", "l0", "w1", "l1", "p", "w1", "l1",
-    "p", "p", "p", "w0", "p", "w0", "w1", "l1", "p", "t",
+    "p", "p", "p", "w0", "p", "w0", "w1", "l1", "t", "p",
     "chain", "w1", "w1", "t", "chain",
 )
 

time: 162 us -> 159 us (0.981)
  Pallas kernels: 160 us -> 158 us
    pallas_call x1, Pallas kernels: 120 us -> 118 us  [gather(): pl.pallas_call(gather_kernel, out_shape=(jax.ShapeDtypeStruct((16, 96, 25...]
where the time goes in v3:
time: 159 us
  Pallas kernels  158 us (99%)
    pallas_call x1, Pallas kernels, gather(): pl.pallas_call(gather_kernel, out_shape=(jax.ShapeDtypeStruct((16, 96, 25...  118 us
    pallas_call x1, Pallas kernels, product(): pl.pallas_call(product_kernel, out_shape=jax.ShapeDtypeStruct((1280, 2560...  39.4 us

profile of v3, /device:TPU:1, one launch (start us, length us, event | category | flops | bytes accessed | tf_op | source)
XLA Modules:
  0.0 159.1 jit_solution(15556875841755387364)
XLA Ops:
  0.0 1.5 reshape.14.screen_ref
  1.5 118.1 %exchange.1 = (f32[16,96,2560]{2,1,0:T(8,128)}, bf16[1280,1536]{1,0:T(8,128)(2,1)}, bf16[1280,1536]{1,0:T(8,128)(2,1)}, f32[1280,512]{1,0:T(8,128)}) custom-call(f32[192,1280]{1,0:T(8,128)} %bitcast.5, f32[96,2560]{1,0:T(8,128)} %right_ref.1, f32[1,96]{1,0:T(1,128)} %bitcast.7, s32[1,2]{1,0:T(1,128)} %bitcast.6, f32[80,256]{1,0:T(8,128)} %reshape.14.screen_ref), custom_call_target="tpu_custom_call" | custom-call | tf_op jit(solution)/shard_map/exchange/pallas_call | solution.py:568
  119.7 39.4 %product.1 = f32[1280,2560]{1,0:T(8,128)} custom-call(s32[2]{0:T(128)} %index_ref.1, bf16[1280,1536]{1,0:T(8,128)(2,1)} %get-tuple-element.9.lh_ref, bf16[1280,1536]{1,0:T(8,128)(2,1)} %get-tuple-element.10.ll_ref, f32[1536,2560]{1,0:T(8,128)} %bitcast.4, f32[1280,512]{1,0:T(8,128)} %get-tuple-element.12.lower_ref, f32[80,256]{1,0:T(8,128)} %reshape.14.screen_ref), custom_call_target="tpu_custom_call" | custom-call | tf_op jit(solution)/shard_map/product/pallas_call | solution.py:643
